TPU v7x, 256 devices: a whole 4x4x8 slice. The times are simulated.
256 devices in a mesh: row: 16 (over y, x), col: 2 (over core), ctx: 8 (over z).
Axes of the slice: x: 4, y: 4, z: 8, core: 2. Of those that a mesh axis runs over, the one named last changes fastest.
Arguments:
- queries: bfloat16 [8192, 6144], P(('col', 'ctx'), 'row'), may hold values from -16 to 16
- keys: bfloat16 [8192, 6144], P(('col', 'ctx'), 'row'), may hold values from -16 to 16
- values: bfloat16 [8192, 6144], P(('col', 'ctx'), 'row'), may hold values from -6 to 6
- out_weight: bfloat16 [6144, 6144], P('col', 'row'), may hold values from -0.078125 to 0.078125
- cotangent: bfloat16 [8192, 6144], P(('col', 'ctx'), 'row'), may hold values from -0.125 to 0.125
- block_mask: int32 [16, 16], replicated, may hold values from 0 to 1, as said below
Outputs:
- mixed_out: bfloat16 [8192, 6144], P(('col', 'ctx'), 'row')
- grad_weight: bfloat16 [6144, 6144], P(('col', 'ctx'), 'row')
Inputs may be any that keep to these rules, and one draw needn't show every extreme that they name: block_mask[i, i] is 1 for every block i, and block_mask[i, j] is 0 for j > i.
All inputs are finite; a program needn't handle non-finite values.
Results may differ from a plain program's by a relative error of at most 0.013.
Values may be sent and summed in bfloat16 or wider, within the bound.
A program may use at most 64 MiB of HBM per device.

v0:
```python
import math
import jax
import jax.numpy as jnp
from jax import lax
from jax.sharding import PartitionSpec as P

HD = 128
BLOCK = 512
NEGATIVE_FILL = -1e30


def attend_block(carried, query_heads, key_block, value_block, allowed, score_scale):
    run_max, run_sum, weighted = carried
    tok_rows, head_count, head_size = query_heads.shape
    key_heads = key_block.reshape(key_block.shape[0], head_count, head_size)
    value_heads = value_block.reshape(value_block.shape[0], head_count, head_size)
    scores = (
        jnp.einsum("thd,uhd->thu", query_heads, key_heads, preferred_element_type=jnp.float32)
        * score_scale
    )
    scores = jnp.where(allowed[:, None, None], scores, NEGATIVE_FILL)
    new_max = jnp.maximum(run_max, jnp.max(scores, axis=2))
    correction = jnp.exp(run_max - new_max)
    weights = jnp.where(allowed[:, None, None], jnp.exp(scores - new_max[:, :, None]), 0.0)
    new_sum = run_sum * correction + jnp.sum(weights, axis=2)
    product = jnp.einsum(
        "thu,uhd->thd",
        weights.astype(jnp.bfloat16),
        value_heads,
        preferred_element_type=jnp.float32,
    )
    new_weighted = weighted * correction[:, :, None] + product
    return (new_max, new_sum, new_weighted)


def body(queries, keys, values, out_weight, cotangent, block_mask):
    tok_rows, feature_width = queries.shape
    head_count = feature_width // HD
    query_heads = queries.reshape(tok_rows, head_count, HD)
    score_scale = 1.0 / math.sqrt(HD)
    local_blocks = tok_rows // BLOCK
    first_block = lax.axis_index(("col", "ctx")) * local_blocks
    local_mask = lax.dynamic_slice_in_dim(block_mask, first_block, local_blocks, 0)
    start_state = (
        jnp.full((tok_rows, head_count), NEGATIVE_FILL, jnp.float32),
        jnp.zeros((tok_rows, head_count), jnp.float32),
        jnp.zeros((tok_rows, head_count, HD), jnp.float32),
    )
    key_piece = lax.all_gather(keys, ("col", "ctx"), axis=0, tiled=True)
    value_piece = lax.all_gather(values, ("col", "ctx"), axis=0, tiled=True)
    block_count = key_piece.shape[0] // BLOCK
    key_stack = key_piece.reshape(block_count, BLOCK, feature_width)
    value_stack = value_piece.reshape(block_count, BLOCK, feature_width)
    block_columns = jnp.arange(block_count, dtype=jnp.int32)

    def one_block(state_in, entries):
        key_block, value_block, block_column = entries
        mask_column = lax.dynamic_index_in_dim(local_mask, block_column, 1, keepdims=False)
        allowed = jnp.repeat(mask_column, BLOCK, total_repeat_length=tok_rows) == 1
        updated = attend_block(state_in, query_heads, key_block, value_block, allowed, score_scale)
        return (updated, None)

    state_out, _ = lax.scan(one_block, start_state, (key_stack, value_stack, block_columns))
    run_max, run_sum, weighted = state_out
    attended = (
        (weighted / run_sum[:, :, None]).reshape(tok_rows, feature_width).astype(jnp.bfloat16)
    )
    all_heads = lax.all_gather(attended, "row", axis=1, tiled=True)
    head_columns = all_heads
    mixed_out = jnp.dot(
        head_columns,
        lax.all_gather(out_weight, "col", axis=0, tiled=True),
        preferred_element_type=jnp.float32,
    )
    head_columns = all_heads
    grad_weight = lax.psum_scatter(
        lax.dot_general(
            head_columns, cotangent, (((0,), (0,)), ((), ())), preferred_element_type=jnp.float32
        ),
        ("col", "ctx"),
        scatter_dimension=0,
        tiled=True,
    )
    return (mixed_out.astype(jnp.bfloat16), grad_weight.astype(jnp.bfloat16))


def solution(mesh):
    in_specs = (
        P(("col", "ctx"), "row"),
        P(("col", "ctx"), "row"),
        P(("col", "ctx"), "row"),
        P("col", "row"),
        P(("col", "ctx"), "row"),
        P(),
    )
    out_specs = (P(("col", "ctx"), "row"), P(("col", "ctx"), "row"))
    return jax.shard_map(body, mesh=mesh, in_specs=in_specs, out_specs=out_specs, check_vma=False)
```

profile of v0, /device:TPU:1, one launch (start us, length us, event | category | flops | bytes accessed | tf_op | source)
XLA Modules:
  0.0 622.6 jit_solution(9049366893125646251)
XLA Ops:
  12.0 48.1 %all-gather.5.cloned.1.call-done = bf16[8192,384]{1,0:T(8,128)(2,1)} async-done(((bf16[512,384]{1,0:T(8,128)(2,1)}), bf16[8192,384]{1,0:T(8,128)(2,1)}) %all-gather.5.cloned.1.call-update) | async-done | bytes 6291472 | tf_op jit(solution)/shard_map/all_gather | solution.py:49
  60.1 46.5 %all-gather.7.cloned.1.call-done = bf16[8192,384]{1,0:T(8,128)(2,1)} async-done(((bf16[512,384]{1,0:T(8,128)(2,1)}), bf16[8192,384]{1,0:T(8,128)(2,1)}) %all-gather.7.cloned.1.call-update) | async-done | bytes 6291472 | tf_op jit(solution)/shard_map/all_gather | solution.py:50
  107.2 304.6 %while.22 = (s32[]{:T(128)}, f32[512,3]{0,1:T(4,128)}, f32[512,3]{0,1:T(4,128)}, f32[512,3,128]{0,2,1:T(8,128)}, s32[16]{0:T(128)}, /*index=5*/s32[1,16]{1,0:T(1...) while((s32[]{:T(128)}, f32[512,3]{0,1:T(4,128)}, ...), condition=%wide.region_3.4_spmd.clone, body=%wide.region_0.3_spmd.clone.sunk | while | flops 413474304 | bytes 15433919 | solution.py:63
  111.5 1.9 constant_dynamic-slice_fusion.5
  114.3 2.4 bitcast_reduce_fusion.2
  120.7 3.4 fusion.42
  128.9 1.9 constant_dynamic-slice_fusion.5
  131.8 2.4 bitcast_reduce_fusion.2
  139.5 3.7 fusion.42
  148.1 1.9 constant_dynamic-slice_fusion.5
  151.0 2.4 bitcast_reduce_fusion.2
  158.7 3.7 fusion.42
  167.2 1.9 constant_dynamic-slice_fusion.5
  170.1 2.4 bitcast_reduce_fusion.2
  177.8 3.7 fusion.42
  186.4 1.9 constant_dynamic-slice_fusion.5
  189.2 2.4 bitcast_reduce_fusion.2
  197.0 3.7 fusion.42
  205.5 1.9 constant_dynamic-slice_fusion.5
  208.4 2.4 bitcast_reduce_fusion.2
  216.1 3.7 fusion.42
  227.5 2.4 bitcast_reduce_fusion.2
  235.2 3.7 fusion.42
  246.7 2.4 bitcast_reduce_fusion.2
  254.4 3.7 fusion.42
  265.8 2.4 bitcast_reduce_fusion.2
  273.5 3.7 fusion.42
  284.9 2.4 bitcast_reduce_fusion.2
  292.7 3.7 fusion.42
  304.1 2.4 bitcast_reduce_fusion.2
  311.8 3.7 fusion.42
  323.2 2.4 bitcast_reduce_fusion.2
  330.9 3.7 fusion.42
  342.4 2.4 bitcast_reduce_fusion.2
  350.1 3.7 fusion.42
  361.5 2.4 bitcast_reduce_fusion.2
  369.2 3.7 fusion.42
  380.6 2.4 bitcast_reduce_fusion.2
  388.3 3.7 fusion.42
  396.9 1.9 constant_dynamic-slice_fusion.5
  399.8 2.4 bitcast_reduce_fusion.2
  407.5 3.7 fusion.42
  411.7 2.0 divide_convert_fusion
  414.4 64.1 %all-gather.9.cloned.1.call-done = bf16[512,6144]{0,1:T(8,128)(2,1)} async-done(((bf16[512,384]{0,1:T(8,128)(2,1)}), bf16[512,6144]{0,1:T(8,128)(2,1)}) %all-gather.9.cloned.1.call-update) | async-done | bytes 6291472 | tf_op jit(solution)/shard_map/all_gather | solution.py:68
  478.5 9.9 %fusion.19 = f32[6144,384]{1,0:T(8,128)} fusion(bf16[512,6144]{0,1:T(8,128)(2,1)} %all-gather.9.cloned.1.call-done, bf16[512,384]{1,0:T(8,128)(2,1)S(1)} %copy-done), kind=kOutput, calls=%fused_computation.27 | convolution fusion | flops 2415919104 | bytes 16121856 | tf_op jit(solution)/shard_map/dot_general | solution.py:77
  488.4 12.0 %all-gather.11.cloned.1.call-done = bf16[6144,384]{1,0:T(8,128)(2,1)} async-done(((bf16[3072,384]{1,0:T(8,128)(2,1)}), bf16[6144,384]{1,0:T(8,128)(2,1)}) %all-gather.11.cloned.1.call-update) | async-done | bytes 4718608 | tf_op jit(solution)/shard_map/all_gather | solution.py:72
  500.4 8.3 %convolution_convert_fusion = bf16[512,384]{1,0:T(8,128)(2,1)} fusion(bf16[512,6144]{0,1:T(8,128)(2,1)} %all-gather.9.cloned.1.call-done, bf16[6144,384]{1,0:T(8,128)(2,1)} %all-gather.11.cloned.1.call-done), kind=kOutput, calls=%fused_computation.23 | convolution fusion | flops 2416115712 | bytes 11403264 | tf_op jit(solution)/shard_map/dot_general | solution.py:70
  508.7 105.5 %reduce-scatter.2.cloned.1.call-done = f32[384,384]{1,0:T(8,128)} async-done(((f32[6144,384]{1,0:T(8,128)}), f32[384,384]{1,0:T(8,128)}) %reduce-scatter.2.cloned.1.call-update) | async-done | bytes 589840 | tf_op jit(solution)/shard_map/reduce_scatter | solution.py:76
  (157 shorter events, 172.3 us)
Async XLA Ops:
  7.2 471.3 %copy-start = (bf16[512,384]{1,0:T(8,128)(2,1)S(1)}, bf16[512,384]{1,0:T(8,128)(2,1)}, u32[]{:S(2)}) copy-start(bf16[512,384]{1,0:T(8,128)(2,1)} %param.16) | copy-start | bytes 1179652
  7.2 53.0 %all-gather.5.cloned.1.call-start = ((), (), s32[]{:S(2)}) async-start(), calls=%async_computation.1 | async-start | bytes 6684672 | tf_op jit(solution)/shard_map/all_gather | solution.py:49
  7.9 98.7 %all-gather.7.cloned.1.call-start = ((), (), s32[]{:S(2)}) async-start(), calls=%async_computation.2 | async-start | bytes 6684672 | tf_op jit(solution)/shard_map/all_gather | solution.py:50
  8.7 469.8 %all-gather.9.cloned.1.call-start = ((), (), s32[]{:S(2)}) async-start(), calls=%async_computation.3 | async-start | bytes 6684672 | tf_op jit(solution)/shard_map/all_gather | solution.py:68
  413.7 86.7 %all-gather.11.cloned.1.call-start = ((), (), s32[]{:S(2)}) async-start(), calls=%async_computation.4 | async-start | bytes 7077888 | tf_op jit(solution)/shard_map/all_gather | solution.py:72
  414.3 200.0 %reduce-scatter.2.cloned.1.call-start = ((), (), s32[]{:S(2)}) async-start(), calls=%async_computation.5 | async-start | bytes 10027008 | tf_op jit(solution)/shard_map/reduce_scatter | solution.py:76
Sparse Core Ops, SparseCore 0:
  9.8 50.2 all-gather.4
  62.0 44.6 all-gather.6
  413.9 64.5 all-gather.8
  480.1 20.2 all-gather.10
  502.8 111.4 reduce-scatter.1
where the time goes:
time: 627 us; the launch traced here: 623 us
  waiting for transfers between devices  278 us (44%)
  matrix products  115 us (18%)
  local copies, waits for them, and re-layouts  110 us (18%)
  other arithmetic  75.8 us (12%)
  loops' own time  29.9 us (5%)
  between operations  13.8 us (2%)
    reduce_scatter x1, waiting for transfers between devices, body(): lax.psum_scatter(lax.dot_general(head_columns, cotangent, (((0,), (0,)),...  106 us
    dynamic_slice x64, local copies, waits for them, and re-layouts, body(): lax.scan(one_block, start_state, (key_stack, value_stack, block_columns))  96.5 us
    all_gather x1, waiting for transfers between devices, body(): all_heads = lax.all_gather(attended, 'row', axis=1, tiled=True)  64.1 us
    dot_general x16, matrix products, attend_block(): jnp.einsum('thu,uhd->thd', weights.astype(jnp.bfloat16), value_heads, pre...  58.4 us
    all_gather x1, waiting for transfers between devices, body(): key_piece = lax.all_gather(keys, ('col', 'ctx'), axis=0, tiled=True)  48.1 us
    all_gather x1, waiting for transfers between devices, body(): value_piece = lax.all_gather(values, ('col', 'ctx'), axis=0, tiled=True)  46.5 us
    dot_general x16, matrix products, attend_block(): jnp.einsum('thd,uhd->thu', query_heads, key_heads, preferred_element_type...  38.2 us
    another operation x1, loops' own time, body(): lax.scan(one_block, start_state, (key_stack, value_stack, block_columns))  29.9 us
  transfers between devices with their start and end apart: 5, of which 5 were waited for; matrix products, arithmetic and copies ran while one was open for 3% of the time, Pallas kernels for 0%

commit v1 on v0

--- a/solution.py
+++ b/solution.py
@@ -7,6 +7,14 @@
 HD = 128
 BLOCK = 512
 NEGATIVE_FILL = -1e30
+
+
+def gather_from_all(shard, axis, dim):
+    size = lax.axis_size(axis)
+    repeats = [size if d == dim else 1 for d in range(shard.ndim)]
+    return lax.all_to_all(
+        jnp.tile(shard, repeats), axis, split_axis=dim, concat_axis=dim, tiled=True
+    )
 
 
 def attend_block(carried, query_heads, key_block, value_block, allowed, score_scale):
@@ -47,7 +55,7 @@
         jnp.zeros((tok_rows, head_count, HD), jnp.float32),
     )
     key_piece = lax.all_gather(keys, ("col", "ctx"), axis=0, tiled=True)
-    value_piece = lax.all_gather(values, ("col", "ctx"), axis=0, tiled=True)
+    value_piece = gather_from_all(values, ("col", "ctx"), 0)
     block_count = key_piece.shape[0] // BLOCK
     key_stack = key_piece.reshape(block_count, BLOCK, feature_width)
     value_stack = value_piece.reshape(block_count, BLOCK, feature_width)

time: 627 us -> 624 us (level)
  waiting for transfers between devices: 278 us -> 349 us
  matrix products: 115 us -> 80.3 us
  other arithmetic: 75.8 us -> 46 us
  local copies, waits for them, and re-layouts: 110 us -> 91 us
  starting transfers between devices: 0.19 us -> 10.3 us
    all_to_all x0 -> x1, waiting for transfers between devices: none -> 164 us  [gather_from_all(): lax.all_to_all(jnp.tile(shard, repeats), axis, split_axis=dim, concat_axi...]
    all_gather x1, waiting for transfers between devices: 48.1 us -> 0.01 us  [body(): key_piece = lax.all_gather(keys, ('col', 'ctx'), axis=0, tiled=True)]
    all_gather x1 -> x0, waiting for transfers between devices: 46.5 us -> none  [body(): value_piece = lax.all_gather(values, ('col', 'ctx'), axis=0, tiled=True)]
    dot_general x16, matrix products: 58.4 us -> 24.7 us  [attend_block(): jnp.einsum('thu,uhd->thd', weights.astype(jnp.bfloat16), value_heads, pre...]
    dynamic_slice x64, local copies, waits for them, and re-layouts: 96.5 us -> 69.1 us  [body(): lax.scan(one_block, start_state, (key_stack, value_stack, block_columns))]
    add x16, other arithmetic: 20.6 us -> 0.33 us  [attend_block(): new_sum = run_sum * correction + jnp.sum(weights, axis=2)]
    max x16, other arithmetic: 10.6 us -> 0.11 us  [attend_block(): new_max = jnp.maximum(run_max, jnp.max(scores, axis=2))]
    all_to_all x0 -> x1, starting transfers between devices: none -> 10.1 us  [gather_from_all(): lax.all_to_all(jnp.tile(shard, repeats), axis, split_axis=dim, concat_axi...]
  transfers between devices with their start and end apart: 5 -> 5, of which waited for: 5 -> 4; matrix products, arithmetic and copies ran while one was open for 3% -> 3% of each run, Pallas kernels for 0% -> 0%
where the time goes in v1:
time: 624 us; the launch traced here: 621 us
  waiting for transfers between devices  349 us (56%)
  local copies, waits for them, and re-layouts  91 us (15%)
  matrix products  80.3 us (13%)
  other arithmetic  46 us (7%)
  loops' own time  30.6 us (5%)
  between operations  13.8 us (2%)
  starting transfers between devices  10.3 us (2%)
    all_to_all x1, waiting for transfers between devices, gather_from_all(): lax.all_to_all(jnp.tile(shard, repeats), axis, split_axis=dim, concat_axi...  164 us
    reduce_scatter x1, waiting for transfers between devices, body(): lax.psum_scatter(lax.dot_general(head_columns, cotangent, (((0,), (0,)),...  106 us
    dynamic_slice x64, local copies, waits for them, and re-layouts, body(): lax.scan(one_block, start_state, (key_stack, value_stack, block_columns))  69.1 us
    all_gather x1, waiting for transfers between devices, body(): all_heads = lax.all_gather(attended, 'row', axis=1, tiled=True)  66.3 us
    dot_general x16, matrix products, attend_block(): jnp.einsum('thd,uhd->thu', query_heads, key_heads, preferred_element_type...  37.4 us
    another operation x1, loops' own time, body(): lax.scan(one_block, start_state, (key_stack, value_stack, block_columns))  30.6 us
    dot_general x16, matrix products, attend_block(): jnp.einsum('thu,uhd->thd', weights.astype(jnp.bfloat16), value_heads, pre...  24.7 us
    reduce_sum x16, other arithmetic, attend_block(): new_sum = run_sum * correction + jnp.sum(weights, axis=2)  21.9 us
  transfers between devices with their start and end apart: 5, of which 4 were waited for; matrix products, arithmetic and copies ran while one was open for 3% of the time, Pallas kernels for 0%

profile of v1, /device:TPU:1, one launch (start us, length us, event | category | flops | bytes accessed | tf_op | source)
XLA Modules:
  0.0 621.0 jit_solution(18026039779905775649)
XLA Ops:
  8.4 3.2 tile.2
  11.6 10.1 %all-to-all-start = ((bf16[16,512,384]{1,2,0:T(8,128)(2,1)}), bf16[16,512,384]{1,2,0:T(8,128)(2,1)}, u32[]{:S(2)}, u32[]{:S(2)}) async-start(bf16[16,512,384]{1,2,0:T(8,128)(2,1)} %tile.2), calls=%async_computation | async-start | bytes 12582912 | tf_op jit(solution)/shard_map/all_to_all | solution.py:15
  24.9 163.6 %all-to-all-done = bf16[16,512,384]{1,2,0:T(8,128)(2,1)} async-done(((bf16[16,512,384]{1,2,0:T(8,128)(2,1)}), bf16[16,512,384]{1,2,0:T(8,128)(2,1)}, u32[]{:S(2)}, u32[]{:S(2)}) %all-to-all-start) | async-done | bytes 6291488 | tf_op jit(solution)/shard_map/all_to_all | solution.py:15
  189.1 218.5 %while.22 = (s32[]{:T(128)}, f32[512,3]{0,1:T(4,128)S(1)}, f32[512,3]{0,1:T(4,128)}, f32[512,3,128]{0,2,1:T(8,128)}, s32[16]{0:T(128)}, /*index=5*/s32[1,16]{1,0...) while((s32[]{:T(128)}, f32[512,3]{0,1:T(4,128)S(1)}, ...), condition=%wide.region_3.4_spmd.clone, body=%wide.region_0.3_spmd.clone.sunk | while | flops 413474304 | bytes 20988212 | solution.py:71
  195.4 2.3 bitcast_reduce_fusion.2
  200.3 1.5 fusion.42
  209.1 2.3 bitcast_reduce_fusion.2
  211.5 1.4 fusion.40
  213.9 1.5 fusion.42
  222.8 2.3 bitcast_reduce_fusion.2
  227.6 1.5 fusion.42
  236.4 2.3 bitcast_reduce_fusion.2
  241.3 1.5 fusion.42
  250.1 2.3 bitcast_reduce_fusion.2
  254.9 1.5 fusion.42
  263.7 2.3 bitcast_reduce_fusion.2
  266.1 1.4 fusion.40
  268.6 1.5 fusion.42
  277.4 2.3 bitcast_reduce_fusion.2
  282.2 1.5 fusion.42
  291.1 2.3 bitcast_reduce_fusion.2
  293.4 1.4 fusion.40
  295.9 1.5 fusion.42
  304.7 2.3 bitcast_reduce_fusion.2
  309.6 1.5 fusion.42
  318.4 2.3 bitcast_reduce_fusion.2
  323.2 1.5 fusion.42
  332.0 2.3 bitcast_reduce_fusion.2
  334.4 1.4 fusion.40
  336.9 1.5 fusion.42
  345.7 2.3 bitcast_reduce_fusion.2
  350.5 1.5 fusion.42
  359.3 2.3 bitcast_reduce_fusion.2
  364.2 1.5 fusion.42
  373.0 2.3 bitcast_reduce_fusion.2
  375.4 1.4 fusion.40
  377.8 1.5 fusion.42
  386.7 2.3 bitcast_reduce_fusion.2
  391.5 1.5 fusion.42
  400.3 2.3 bitcast_reduce_fusion.2
  405.2 1.5 fusion.42
  407.6 2.0 divide_convert_fusion
  410.4 66.3 %all-gather.6.cloned.1.call-done = bf16[512,6144]{0,1:T(8,128)(2,1)} async-done(((bf16[512,384]{0,1:T(8,128)(2,1)}), bf16[512,6144]{0,1:T(8,128)(2,1)}) %all-gather.6.cloned.1.call-update) | async-done | bytes 6291472 | tf_op jit(solution)/shard_map/all_gather | solution.py:76
  476.7 9.9 %fusion.19 = f32[6144,384]{1,0:T(8,128)} fusion(bf16[512,6144]{0,1:T(8,128)(2,1)} %all-gather.6.cloned.1.call-done, bf16[512,384]{1,0:T(8,128)(2,1)S(1)} %copy-done), kind=kOutput, calls=%fused_computation.27 | convolution fusion | flops 2415919104 | bytes 16121856 | tf_op jit(solution)/shard_map/dot_general | solution.py:85
  486.6 12.2 %all-gather.8.cloned.1.call-done = bf16[6144,384]{1,0:T(8,128)(2,1)} async-done(((bf16[3072,384]{1,0:T(8,128)(2,1)}), bf16[6144,384]{1,0:T(8,128)(2,1)}) %all-gather.8.cloned.1.call-update) | async-done | bytes 4718608 | tf_op jit(solution)/shard_map/all_gather | solution.py:80
  498.8 8.3 %convolution_convert_fusion = bf16[512,384]{1,0:T(8,128)(2,1)} fusion(bf16[512,6144]{0,1:T(8,128)(2,1)} %all-gather.6.cloned.1.call-done, bf16[6144,384]{1,0:T(8,128)(2,1)} %all-gather.8.cloned.1.call-done), kind=kOutput, calls=%fused_computation.23 | convolution fusion | flops 2416115712 | bytes 11403264 | tf_op jit(solution)/shard_map/dot_general | solution.py:78
  507.1 105.5 %reduce-scatter.2.cloned.1.call-done = f32[384,384]{1,0:T(8,128)} async-done(((f32[6144,384]{1,0:T(8,128)}), f32[384,384]{1,0:T(8,128)}) %reduce-scatter.2.cloned.1.call-update) | async-done | bytes 589840 | tf_op jit(solution)/shard_map/reduce_scatter | solution.py:84
  612.7 1.8 convert_element_type.25
  (288 shorter events, 124.8 us)
Async XLA Ops:
  7.2 469.6 %copy-start = (bf16[512,384]{1,0:T(8,128)(2,1)S(1)}, bf16[512,384]{1,0:T(8,128)(2,1)}, u32[]{:S(2)}) copy-start(bf16[512,384]{1,0:T(8,128)(2,1)} %param.16) | copy-start | bytes 1179652
  11.6 10.9 %copy-start.3 = (bf16[512,384]{1,0:T(8,128)(2,1)S(1)}, bf16[512,384]{1,0:T(8,128)(2,1)}, u32[]{:S(2)}) copy-start(bf16[512,384]{1,0:T(8,128)(2,1)} %param.12) | copy-start | bytes 1179652
  11.6 176.9 %all-to-all-start = ((bf16[16,512,384]{1,2,0:T(8,128)(2,1)}), bf16[16,512,384]{1,2,0:T(8,128)(2,1)}, u32[]{:S(2)}, u32[]{:S(2)}) async-start(bf16[16,512,384]{1,2,0:T(8,128)(2,1)} %tile.2), calls=%async_computation | async-start | bytes 12582912 | tf_op jit(solution)/shard_map/all_to_all | solution.py:15
  21.7 166.8 %all-gather.4.cloned.1.call-start = ((), (), s32[]{:S(2)}) async-start(), calls=%async_computation.2 | async-start | bytes 6684672 | tf_op jit(solution)/shard_map/all_gather | solution.py:57
  22.5 454.3 %all-gather.6.cloned.1.call-start = ((), (), s32[]{:S(2)}) async-start(), calls=%async_computation.3 | async-start | bytes 6684672 | tf_op jit(solution)/shard_map/all_gather | solution.py:76
  197.8 1.4 copy-start.4
  197.8 2.5 copy-start.1
  199.2 2.6 copy-start.5
  211.4 1.4 copy-start.4
  211.5 2.5 copy-start.1
  212.9 2.6 copy-start.5
  225.1 1.4 copy-start.4
  225.1 2.5 copy-start.1
  226.5 2.6 copy-start.5
  238.8 1.4 copy-start.4
  238.8 2.5 copy-start.1
  240.2 2.6 copy-start.5
  252.4 1.4 copy-start.4
  252.4 2.5 copy-start.1
  253.9 2.6 copy-start.5
  266.1 1.4 copy-start.4
  266.1 2.5 copy-start.1
  267.5 2.6 copy-start.5
  279.7 1.4 copy-start.4
  279.8 2.5 copy-start.1
  281.2 2.6 copy-start.5
  293.4 1.4 copy-start.4
  293.4 2.5 copy-start.1
  294.8 2.6 copy-start.5
  307.1 1.4 copy-start.4
  307.1 2.5 copy-start.1
  308.5 2.6 copy-start.5
  320.7 2.5 copy-start.1
  322.2 2.6 copy-start.5
  334.4 2.5 copy-start.1
  335.8 2.6 copy-start.5
  348.0 2.5 copy-start.1
  349.5 2.6 copy-start.5
  361.7 2.5 copy-start.1
  363.1 2.6 copy-start.5
  375.4 2.5 copy-start.1
  376.8 2.6 copy-start.5
  389.0 2.5 copy-start.1
  390.5 2.6 copy-start.5
  402.7 2.5 copy-start.1
  404.1 2.6 copy-start.5
  409.6 89.2 %all-gather.8.cloned.1.call-start = ((), (), s32[]{:S(2)}) async-start(), calls=%async_computation.4 | async-start | bytes 7077888 | tf_op jit(solution)/shard_map/all_gather | solution.py:80
  410.4 202.3 %reduce-scatter.2.cloned.1.call-start = ((), (), s32[]{:S(2)}) async-start(), calls=%async_computation.5 | async-start | bytes 10027008 | tf_op jit(solution)/shard_map/reduce_scatter | solution.py:84
  (23 other events, 24.3 us)
Sparse Core Ops, SparseCore 0:
  24.4 152.5 all-gather.3
  409.7 66.9 all-gather.5
  478.5 20.2 all-gather.7
  501.2 111.4 reduce-scatter.1
